TPU v7x, 32 devices: a whole 2x2x4 slice. The times are simulated.
32 devices in a mesh: row: 8 (over y, x, core), col: 4 (over z).
Axes of the slice: x: 2, y: 2, z: 4, core: 2. Of those that a mesh axis runs over, the one named last changes fastest.
Arguments:
- upper_s: float32 [4, 2048, 8, 1024], P(None, 'row', None, 'col')
- upper_t: float32 [4, 2048, 8, 1024], P(None, 'row', None, 'col')
- left_vectors: float32 [4, 2048, 8, 1024], P(None, 'row', None, 'col'), may hold values from -6 to 6
- right_vectors: float32 [4, 2048, 8, 1024], P(None, 'row', None, 'col'), may hold values from -6 to 6
- window_starts: int32 [3, 16], replicated, may hold values from 0 to 31, as said below
- selection: int32 [3, 16, 256], replicated, may hold values 0 or 1
- window_factors: float32 [3, 16, 2, 256, 256], P(None, 'row')
Outputs:
- new_s: float32 [4, 2048, 8, 1024], P(None, 'row', None, 'col')
- new_t: float32 [4, 2048, 8, 1024], P(None, 'row', None, 'col')
- new_left: float32 [4, 2048, 8, 1024], P(None, 'row', None, 'col')
- new_right: float32 [4, 2048, 8, 1024], P(None, 'row', None, 'col')
Inputs may be any that keep to these rules, and one draw needn't show every extreme that they name: `window_starts`: within each round the 16 block numbers are distinct.
All inputs are finite; a program needn't handle non-finite values.
Results may differ from a plain program's by a relative error of at most 0.0001.
Values sent between devices are 32-bit elements; how exact they have to be, the bound alone decides.
No kernel may reach another device: no remote copies, remote signals or barrier semaphores. Data moves between devices by JAX's collectives and lax.ppermute only.
A program may use at most 192 MiB of HBM per device.

v0:
```python
import jax
import jax.numpy as jnp
from jax import lax
from jax.sharding import PartitionSpec as P


def destinations(flags):
    earlier = jnp.cumsum(flags) - flags
    chosen = jnp.sum(flags)
    position = jnp.arange(flags.shape[0], dtype=jnp.int32)
    return jnp.where(flags == 1, earlier, chosen + position - earlier)


def window_bases(factors, flags):
    target = destinations(flags)
    return (jnp.take(factors[0], target, axis=0), jnp.take(factors[1], target, axis=0))


def fill_identity(starts, blocks, chosen):
    covered = jnp.sum((blocks[:, None] == starts[None, :]).astype(jnp.float32), axis=1)
    order_w = chosen.shape[1]
    return chosen + (1.0 - covered)[:, None, None] * jnp.eye(order_w, dtype=jnp.float32)


def rows_update(factor, matrix):
    return jnp.einsum("aij,aibl->ajbl", factor, matrix, precision=lax.Precision.HIGHEST)


def cols_update(matrix, factor):
    return jnp.einsum("aibm,bml->aibl", matrix, factor, precision=lax.Precision.HIGHEST)


def slot_factors(own_factors, own_starts, own_flags, starts, row_blocks, col_blocks):
    left_own, right_own = jax.vmap(window_bases)(own_factors, own_flags)
    stacked = jnp.stack([left_own, right_own], axis=1)
    placing = (col_blocks[:, None] == own_starts[None, :]).astype(jnp.float32)
    slots = jnp.einsum("jw,wxab->jxab", placing, stacked, precision=lax.Precision.HIGHEST)
    received = lax.psum(slots, "row")
    picking = (row_blocks[:, None] == col_blocks[None, :]).astype(jnp.float32)
    row_part = jnp.einsum("kj,jab->kab", picking, received[:, 0], precision=lax.Precision.HIGHEST)
    row_sum = lax.psum(row_part, "col")
    left_rows = fill_identity(starts, row_blocks, row_sum)
    left_cols = fill_identity(starts, col_blocks, received[:, 0])
    right_cols = fill_identity(starts, col_blocks, received[:, 1])
    return (left_rows, left_cols, right_cols)


def shards(upper_s, upper_t, left_vectors, right_vectors, window_starts, selection, window_factors):
    row_index = lax.axis_index("row")
    col_index = lax.axis_index("col")
    row_count = lax.axis_size("row")
    col_count = lax.axis_size("col")
    local_rows = upper_s.shape[0]
    local_cols = upper_s.shape[2]
    round_count = window_starts.shape[0]
    own_count = window_factors.shape[1]
    row_blocks = jnp.arange(local_rows, dtype=jnp.int32) * row_count + row_index
    col_blocks = jnp.arange(local_cols, dtype=jnp.int32) * col_count + col_index
    for round_idx in range(round_count):
        starts = window_starts[round_idx]
        first = row_index * own_count
        own_starts = lax.dynamic_slice_in_dim(starts, first, own_count, 0)
        own_flags = lax.dynamic_slice_in_dim(selection[round_idx], first, own_count, 0)
        left_rows, left_cols, right_cols = slot_factors(
            window_factors[round_idx], own_starts, own_flags, starts, row_blocks, col_blocks
        )
        upper_s = cols_update(rows_update(left_rows, upper_s), right_cols)
        upper_t = cols_update(rows_update(left_rows, upper_t), right_cols)
        left_vectors = cols_update(left_vectors, left_cols)
        right_vectors = cols_update(right_vectors, right_cols)
    return (upper_s, upper_t, left_vectors, right_vectors)


def solution(mesh):
    return jax.shard_map(
        shards,
        mesh=mesh,
        in_specs=(
            P(None, "row", None, "col"),
            P(None, "row", None, "col"),
            P(None, "row", None, "col"),
            P(None, "row", None, "col"),
            P(),
            P(),
            P(None, "row", None, None, None),
        ),
        out_specs=(
            P(None, "row", None, "col"),
            P(None, "row", None, "col"),
            P(None, "row", None, "col"),
            P(None, "row", None, "col"),
        ),
        check_vma=False,
    )
```

profile of v0, /device:TPU:0, one launch (start us, length us, event | category | flops | bytes accessed | tf_op | source)
XLA Modules:
  0.0 584.6 jit_solution(2492521393092527794)
XLA Ops:
  12.0 6.4 %gather_fusion = f32[512,256]{1,0:T(8,128)} fusion(f32[2,256,256]{2,1,0:T(8,128)S(1)} %get-tuple-element.58, s32[512]{0:T(512)S(1)} %bitcast.239), kind=kCustom, calls=%fused_computation.clone | custom fusion | bytes 1052672 | tf_op jit(solution)/shard_map/vmap(jit(_take))/gather | solution.py:16
  18.4 6.4 %gather_fusion.1 = f32[512,256]{1,0:T(8,128)} fusion(f32[2,256,256]{2,1,0:T(8,128)S(1)} %get-tuple-element.59, s32[512]{0:T(512)S(1)} %bitcast.240), kind=kCustom, calls=%fused_computation.1.clone | custom fusion | bytes 1052672 | tf_op jit(solution)/shard_map/vmap(jit(_take))/gather | solution.py:16
  29.0 6.4 %gather_fusion.2 = f32[512,256]{1,0:T(8,128)} fusion(f32[2,256,256]{2,1,0:T(8,128)S(1)} %get-tuple-element.56, s32[512]{0:T(512)S(1)} %bitcast.243), kind=kCustom, calls=%fused_computation.2.clone | custom fusion | bytes 1052672 | tf_op jit(solution)/shard_map/vmap(jit(_take))/gather | solution.py:16
  35.3 6.4 %gather_fusion.3 = f32[512,256]{1,0:T(8,128)} fusion(f32[2,256,256]{2,1,0:T(8,128)S(1)} %get-tuple-element.57, s32[512]{0:T(512)S(1)} %bitcast.244), kind=kCustom, calls=%fused_computation.3.clone | custom fusion | bytes 1052672 | tf_op jit(solution)/shard_map/vmap(jit(_take))/gather | solution.py:16
  54.1 4.3 fusion.42
  58.4 4.3 fusion.46
  63.9 15.0 %fusion.50 = f32[8,2,256,256]{3,0,2,1:T(8,128)} fusion(f32[2,1,256,256]{3,0,2,1:T(2,128)S(1)} %get-tuple-element.68, f32[2,1,256,256]{3,0,2,1:T(2,128)S(1)} %get-tuple-element.67, s32[8]{0:T(128)S(1)} %multiply_add_fusion.16, s32[2]{0:T(128)S(1)} %fusion.102), kind=kOutput, calls=%fused_computation.66 | convolution fusion | flops 25427984 | bytes 5242920 | tf_op jit(solution)/shard_map/jw,wxab->jxab/dot_general | solution.py:37
  79.4 174.4 %all-reduce.5.cloned.1.call-done = (f32[8,2,256,256]{3,0,2,1:T(8,128)}, f32[8,2,256,256]{3,0,2,1:T(8,128)}, f32[8,2,256,256]{3,0,2,1:T(8,128)}) async-done(((f32[8,2,256,256]{3,0,2,1:T(8,128)}, f32[8,2,256,256]{3,0,2,1:T(8,128)}, f32[8,2,256,256]{3,0,2,1:T(8,128)}), (f32[8,2,256,256]{3,0,2,1:T(8,128)}, f32[8,2,256,256]{3,0,2,1:T(8,128)}, f32[8,2,256,256]{3,0,2,1:T(8,128)})) %all-reduce.5.cloned.1.call-update) | async-done | bytes 12582928 | tf_op jit(solution)/shard_map/psum | solution.py:38
  264.0 8.5 %fusion.31 = (f32[8,256,256,1]{2,0,1,3:T(8,128)}, f32[8,256,256,1]{2,0,1,3:T(8,128)}, f32[8,256,256,1]{2,0,1,3:T(8,128)}, f32[8,256,256,1]{2,0,1,3:T(8,128)S(1)}...) fusion(f32[8,2,256,256]{3,0,2,1:T(8,128)} %get-tuple-element.27, f32[256,256]{1,0:T(8,128)S(1)} %fusion.78, ...), kind=kLoop, calls=%fused_computation.41 | loop fusion | flops 4718592 | bytes 25428064 | tf_op jit(solution)/shard_map/add | solution.py:22
  272.5 21.2 %fusion.22 = f32[8,256,4,256]{3,1,2,0:T(8,128)} fusion(f32[4,256,8,256]{3,2,1,0:T(8,128)} %param.11, f32[8,256,256,1]{2,0,1,3:T(8,128)S(1)} %get-tuple-element.61), kind=kOutput, calls=%fused_computation.28 | convolution fusion | flops 6442450944 | bytes 18874368 | tf_op jit(solution)/shard_map/aibm,bml->aibl/dot_general | solution.py:30
  293.8 12.7 %fusion.6 = f32[8,256,4,256]{3,1,2,0:T(8,128)} fusion(f32[8,256,4,256]{3,1,2,0:T(8,128)} %fusion.22, f32[8,256,256,1]{2,0,1,3:T(8,128)S(1)} %get-tuple-element.63), kind=kOutput, calls=%fused_computation.12 | convolution fusion | flops 6442450944 | bytes 18874368 | tf_op jit(solution)/shard_map/aibm,bml->aibl/dot_general | solution.py:30
  314.3 15.9 %fusion.24 = f32[4,256,8,256]{1,3,0,2:T(8,128)} fusion(f32[8,256,4,256]{3,1,2,0:T(8,128)} %fusion.6, f32[8,256,256,1]{2,0,1,3:T(8,128)} %get-tuple-element.45), kind=kOutput, calls=%fused_computation.30 | convolution fusion | flops 6442450944 | bytes 18874368 | tf_op jit(solution)/shard_map/aibm,bml->aibl/dot_general | solution.py:30
  330.1 10.4 %copy.155 = f32[4,256,8,256]{3,2,1,0:T(8,128)} copy(f32[4,256,8,256]{1,3,0,2:T(8,128)} %fusion.24) | data formatting | bytes 16777216
  340.5 14.8 %fusion.20 = f32[8,256,4,256]{3,1,2,0:T(8,128)S(1)} fusion(f32[8,256,256,1]{1,2,3,0:T(8,128)} %copy.163, f32[4,256,8,256]{3,2,1,0:T(8,128)} %param.12), kind=kOutput, calls=%fused_computation.26 | convolution fusion | flops 6442450944 | bytes 18874368 | tf_op jit(solution)/shard_map/aibm,bml->aibl/dot_general | solution.py:30
  355.4 8.8 %fusion.2 = f32[8,256,4,256]{3,1,2,0:T(8,128)S(1)} fusion(f32[8,256,256,1]{1,2,3,0:T(8,128)S(1)} %copy-done, f32[8,256,4,256]{3,1,2,0:T(8,128)S(1)} %fusion.20), kind=kOutput, calls=%fused_computation.8 | convolution fusion | flops 6442450944 | bytes 18874368 | tf_op jit(solution)/shard_map/aibm,bml->aibl/dot_general | solution.py:30
  364.2 9.8 %fusion.27 = f32[4,256,8,256]{1,3,0,2:T(8,128)} fusion(f32[8,256,256,1]{1,2,3,0:T(8,128)S(1)} %copy.170, f32[8,256,4,256]{3,1,2,0:T(8,128)S(1)} %fusion.2), kind=kOutput, calls=%fused_computation.31 | convolution fusion | flops 6442450944 | bytes 18874368 | tf_op jit(solution)/shard_map/aibm,bml->aibl/dot_general | solution.py:30
  374.0 10.4 %copy.156 = f32[4,256,8,256]{3,2,1,0:T(8,128)} copy(f32[4,256,8,256]{1,3,0,2:T(8,128)} %fusion.27) | data formatting | bytes 16777216
  384.4 30.7 %all-reduce.7.cloned.1.call-done = (f32[4,256,256]{2,1,0:T(8,128)}, f32[4,256,256]{2,1,0:T(8,128)}, f32[4,256,256]{2,1,0:T(8,128)}) async-done(((f32[4,256,256]{2,1,0:T(8,128)}, f32[4,256,256]{2,1,0:T(8,128)}, f32[4,256,256]{2,1,0:T(8,128)}), (f32[4,256,256]{2,1,0:T(8,128)}, f32[4,256,256]{2,1,0:T(8,128)}, f32[4,256,256]{2,1,0:T(8,128)})) %all-reduce.7.cloned.1.call-update) | async-done | bytes 3145744 | tf_op jit(solution)/shard_map/psum | solution.py:41
  415.1 14.4 %fusion.18 = f32[4,256,8,256]{3,1,0,2:T(8,128)S(1)} fusion(f32[4,256,8,256]{3,2,1,0:T(8,128)} %param.9, f32[4,256,256]{2,1,0:T(8,128)} %get-tuple-element.30, f32[4]{0:T(128)S(1)} %get-tuple-element.87, f32[256,256]{1,0:T(8,128)S(1)} %fusion.78), kind=kOutput, calls=%fused_computation.24 | convolution fusion | flops 6442975232 | bytes 18087952 | tf_op jit(solution)/shard_map/aij,aibl->ajbl/dot_general | solution.py:26
  429.5 8.9 %fusion.117 = f32[8,256,4,256]{3,1,2,0:T(8,128)S(1)} fusion(f32[8,256,256,1]{1,2,3,0:T(8,128)S(1)} %copy-done.3, f32[4,256,8,256]{3,1,0,2:T(8,128)S(1)} %fusion.18), kind=kOutput, calls=%fused_computation.194 | convolution fusion | flops 6442450944 | bytes 18874368 | tf_op jit(solution)/shard_map/aibm,bml->aibl/dot_general | solution.py:30
  438.4 14.3 %fusion.16 = f32[4,256,8,256]{3,1,0,2:T(8,128)S(1)} fusion(f32[8,256,4,256]{3,1,2,0:T(8,128)S(1)} %fusion.117, f32[4,256,256]{2,1,0:T(8,128)S(1)} %copy-done.7, f32[4]{0:T(128)S(1)} %get-tuple-element.88, f32[256,256]{1,0:T(8,128)S(1)} %fusion.78), kind=kOutput, calls=%fused_computation.22 | convolution fusion | flops 6442975232 | bytes 18087952 | tf_op jit(solution)/shard_map/aij,aibl->ajbl/dot_general | solution.py:26
  452.7 9.3 %fusion.118 = f32[8,256,4,256]{3,1,2,0:T(8,128)S(1)} fusion(f32[8,256,256,1]{1,2,3,0:T(8,128)S(1)} %copy-done.1, f32[4,256,8,256]{3,1,0,2:T(8,128)S(1)} %fusion.16), kind=kOutput, calls=%fused_computation.195 | convolution fusion | flops 6442450944 | bytes 18874368 | tf_op jit(solution)/shard_map/aibm,bml->aibl/dot_general | solution.py:30
  462.0 14.2 %fusion.14 = f32[4,256,8,256]{3,1,0,2:T(8,128)S(1)} fusion(f32[8,256,4,256]{3,1,2,0:T(8,128)S(1)} %fusion.118, f32[4,256,256]{2,1,0:T(8,128)S(1)} %copy-done.6, f32[256,256]{1,0:T(8,128)S(1)} %fusion.78, f32[4]{0:T(128)S(1)} %broadcast_subtract_fusion.2), kind=kOutput, calls=%fused_computation.20 | convolution fusion | flops 6442975232 | bytes 18087952 | tf_op jit(solution)/shard_map/aij,aibl->ajbl/dot_general | solution.py:26
  476.3 9.7 %convolution_bitcast_fusion.1 = f32[4,256,8,256]{1,3,0,2:T(8,128)} fusion(f32[8,256,256,1]{1,2,3,0:T(8,128)S(1)} %copy.170, f32[4,256,8,256]{3,1,0,2:T(8,128)S(1)} %fusion.14), kind=kOutput, calls=%fused_computation.33 | convolution fusion | flops 6442450944 | bytes 18874368 | tf_op jit(solution)/shard_map/aibm,bml->aibl/dot_general | solution.py:30
  486.0 10.4 %copy.153 = f32[4,256,8,256]{3,2,1,0:T(8,128)} copy(f32[4,256,8,256]{1,3,0,2:T(8,128)} %convolution_bitcast_fusion.1) | data formatting | bytes 16777216
  496.4 14.4 %fusion.12 = f32[4,256,8,256]{3,1,0,2:T(8,128)S(1)} fusion(f32[4,256,8,256]{3,2,1,0:T(8,128)} %param.10, f32[4,256,256]{2,1,0:T(8,128)} %get-tuple-element.30, f32[4]{0:T(128)S(1)} %get-tuple-element.87, f32[256,256]{1,0:T(8,128)S(1)} %fusion.78), kind=kOutput, calls=%fused_computation.18 | convolution fusion | flops 6442975232 | bytes 18087952 | tf_op jit(solution)/shard_map/aij,aibl->ajbl/dot_general | solution.py:26
  510.8 8.9 %fusion.119 = f32[8,256,4,256]{3,1,2,0:T(8,128)S(1)} fusion(f32[8,256,256,1]{1,2,3,0:T(8,128)S(1)} %copy-done.4, f32[4,256,8,256]{3,1,0,2:T(8,128)S(1)} %fusion.12), kind=kOutput, calls=%fused_computation.196 | convolution fusion | flops 6442450944 | bytes 18874368 | tf_op jit(solution)/shard_map/aibm,bml->aibl/dot_general | solution.py:30
  519.7 14.3 %fusion.10 = f32[4,256,8,256]{3,1,0,2:T(8,128)S(1)} fusion(f32[8,256,4,256]{3,1,2,0:T(8,128)S(1)} %fusion.119, f32[4,256,256]{2,1,0:T(8,128)S(1)} %copy-done.8, f32[4]{0:T(128)S(1)} %get-tuple-element.88, f32[256,256]{1,0:T(8,128)S(1)} %fusion.78), kind=kOutput, calls=%fused_computation.16 | convolution fusion | flops 6442975232 | bytes 18087952 | tf_op jit(solution)/shard_map/aij,aibl->ajbl/dot_general | solution.py:26
  534.0 9.3 %fusion.120 = f32[8,256,4,256]{3,1,2,0:T(8,128)S(1)} fusion(f32[8,256,256,1]{1,2,3,0:T(8,128)S(1)} %copy-done.2, f32[4,256,8,256]{3,1,0,2:T(8,128)S(1)} %fusion.10), kind=kOutput, calls=%fused_computation.197 | convolution fusion | flops 6442450944 | bytes 18874368 | tf_op jit(solution)/shard_map/aibm,bml->aibl/dot_general | solution.py:30
  543.3 14.2 %fusion.8 = f32[4,256,8,256]{3,1,0,2:T(8,128)S(1)} fusion(f32[8,256,4,256]{3,1,2,0:T(8,128)S(1)} %fusion.120, f32[4,256,256]{2,1,0:T(8,128)S(1)} %copy-done.6, f32[256,256]{1,0:T(8,128)S(1)} %fusion.78, f32[4]{0:T(128)S(1)} %broadcast_subtract_fusion.2), kind=kOutput, calls=%fused_computation.14 | convolution fusion | flops 6442975232 | bytes 18087952 | tf_op jit(solution)/shard_map/aij,aibl->ajbl/dot_general | solution.py:26
  557.5 9.7 %convolution_bitcast_fusion = f32[4,256,8,256]{1,3,0,2:T(8,128)} fusion(f32[8,256,256,1]{1,2,3,0:T(8,128)S(1)} %copy.170, f32[4,256,8,256]{3,1,0,2:T(8,128)S(1)} %fusion.8), kind=kOutput, calls=%fused_computation.32 | convolution fusion | flops 6442450944 | bytes 18874368 | tf_op jit(solution)/shard_map/aibm,bml->aibl/dot_general | solution.py:30
  567.2 10.4 %copy.154 = f32[4,256,8,256]{3,2,1,0:T(8,128)} copy(f32[4,256,8,256]{1,3,0,2:T(8,128)} %convolution_bitcast_fusion) | data formatting | bytes 16777216
  (94 shorter events, 40.9 us)
Async XLA Ops:
  7.2 3.3 copy-start.12
  7.2 246.6 %all-reduce.5.cloned.1.call-start = ((), (), s32[]{:S(2)}) async-start(), calls=%async_computation | async-start | bytes 25165824 | tf_op jit(solution)/shard_map/psum | solution.py:38
  10.3 14.5 %copy-start.13 = (s32[3,16]{1,0:T(4,128)S(1)}, s32[3,16]{1,0:T(4,128)}, u32[]{:S(2)}) copy-start(s32[3,16]{1,0:T(4,128)} %param.13) | copy-start | bytes 580
  35.3 14.7 %copy-start.9 = (f32[512,256]{1,0:T(8,128)S(1)}, f32[512,256]{1,0:T(8,128)}, u32[]{:S(2)}) copy-start(f32[512,256]{1,0:T(8,128)} %gather_fusion) | copy-start | bytes 1572868
  35.3 14.7 %copy-start.10 = (f32[512,256]{1,0:T(8,128)S(1)}, f32[512,256]{1,0:T(8,128)}, u32[]{:S(2)}) copy-start(f32[512,256]{1,0:T(8,128)} %gather_fusion.1) | copy-start | bytes 1572868
  41.8 9.4 %copy-start.11 = (f32[512,256]{1,0:T(8,128)S(1)}, f32[512,256]{1,0:T(8,128)}, u32[]{:S(2)}) copy-start(f32[512,256]{1,0:T(8,128)} %gather_fusion.3) | copy-start | bytes 1572868
  78.9 336.2 %all-reduce.7.cloned.1.call-start = ((), (), s32[]{:S(2)}) async-start(), calls=%async_computation.1 | async-start | bytes 6291456 | tf_op jit(solution)/shard_map/psum | solution.py:41
  253.8 7.9 %copy-start.5 = (f32[8,2,256,256]{3,0,2,1:T(8,128)S(1)}, f32[8,2,256,256]{3,0,2,1:T(8,128)}, u32[]{:S(2)}) copy-start(f32[8,2,256,256]{3,0,2,1:T(8,128)} %get-tuple-element.27) | copy-start | bytes 12582916
  340.5 14.8 %copy-start = (f32[8,256,256,1]{1,2,3,0:T(8,128)S(1)}, f32[8,256,256,1]{1,2,3,0:T(8,128)}, u32[]{:S(2)}) copy-start(f32[8,256,256,1]{1,2,3,0:T(8,128)} %copy.167) | copy-start | bytes 6291460
  415.1 14.4 %copy-start.3 = (f32[8,256,256,1]{1,2,3,0:T(8,128)S(1)}, f32[8,256,256,1]{1,2,3,0:T(8,128)}, u32[]{:S(2)}) copy-start(f32[8,256,256,1]{1,2,3,0:T(8,128)} %copy.163) | copy-start | bytes 6291460
  429.5 8.9 %copy-start.7 = (f32[4,256,256]{2,1,0:T(8,128)S(1)}, f32[4,256,256]{2,1,0:T(8,128)}, u32[]{:S(2)}) copy-start(f32[4,256,256]{2,1,0:T(8,128)} %get-tuple-element.31) | copy-start | bytes 3145732
  438.4 14.3 %copy-start.1 = (f32[8,256,256,1]{1,2,3,0:T(8,128)S(1)}, f32[8,256,256,1]{1,2,3,0:T(8,128)}, u32[]{:S(2)}) copy-start(f32[8,256,256,1]{1,2,3,0:T(8,128)} %copy.167) | copy-start | bytes 6291460
  452.7 9.3 %copy-start.6 = (f32[4,256,256]{2,1,0:T(8,128)S(1)}, f32[4,256,256]{2,1,0:T(8,128)}, u32[]{:S(2)}) copy-start(f32[4,256,256]{2,1,0:T(8,128)} %get-tuple-element.32) | copy-start | bytes 3145732
  496.4 14.4 %copy-start.4 = (f32[8,256,256,1]{1,2,3,0:T(8,128)S(1)}, f32[8,256,256,1]{1,2,3,0:T(8,128)}, u32[]{:S(2)}) copy-start(f32[8,256,256,1]{1,2,3,0:T(8,128)} %copy.163) | copy-start | bytes 6291460
  510.8 8.9 %copy-start.8 = (f32[4,256,256]{2,1,0:T(8,128)S(1)}, f32[4,256,256]{2,1,0:T(8,128)}, u32[]{:S(2)}) copy-start(f32[4,256,256]{2,1,0:T(8,128)} %get-tuple-element.31) | copy-start | bytes 3145732
  519.7 14.3 %copy-start.2 = (f32[8,256,256,1]{1,2,3,0:T(8,128)S(1)}, f32[8,256,256,1]{1,2,3,0:T(8,128)}, u32[]{:S(2)}) copy-start(f32[8,256,256,1]{1,2,3,0:T(8,128)} %copy.167) | copy-start | bytes 6291460
Sparse Core Ops, SparseCore 0:
  79.0 174.7 all-reduce.4
  293.9 121.1 all-reduce.6
where the time goes:
time: 594 us; the launch traced here: 585 us
  matrix products  255 us (43%)
  waiting for transfers between devices  205 us (35%)
  local copies, waits for them, and re-layouts  92.4 us (16%)
  other arithmetic  17.4 us (3%)
  between operations  14.7 us (2%)
    psum x1, waiting for transfers between devices, slot_factors(): received = lax.psum(slots, 'row')  174 us
    dot_general x12, matrix products, cols_update(): jnp.einsum('aibm,bml->aibl', matrix, factor, precision=lax.Precision.HIGH...  139 us
    dot_general x6, matrix products, rows_update(): jnp.einsum('aij,aibl->ajbl', factor, matrix, precision=lax.Precision.HIGH...  85.8 us
    unnamed x36, local copies, waits for them, and re-layouts  41.7 us
    psum x1, waiting for transfers between devices, slot_factors(): row_sum = lax.psum(row_part, 'col')  30.7 us
    dot_general x3, matrix products, slot_factors(): jnp.einsum('jw,wxab->jxab', placing, stacked, precision=lax.Precision.HIG...  23.5 us
    gather x3, local copies, waits for them, and re-layouts, window_bases(): jnp.take(factors[0], target, axis=0)  16.7 us
    gather x3, local copies, waits for them, and re-layouts, window_bases(): jnp.take(factors[1], target, axis=0)  16.6 us
  transfers between devices with their start and end apart: 2, of which 2 were waited for; matrix products, arithmetic and copies ran while one was open for 16% of the time, Pallas kernels for 0%

commit v1 on v0

--- a/solution.py
+++ b/solution.py
@@ -35,7 +35,10 @@
     stacked = jnp.stack([left_own, right_own], axis=1)
     placing = (col_blocks[:, None] == own_starts[None, :]).astype(jnp.float32)
     slots = jnp.einsum("jw,wxab->jxab", placing, stacked, precision=lax.Precision.HIGHEST)
-    received = lax.psum(slots, "row")
+    size, received = (lax.axis_size("row"), slots)
+    for stride in [1 << k for k in range(size.bit_length() - 1)]:
+        route = [(i, i ^ stride) for i in range(size)]
+        received = received + lax.ppermute(received, "row", route)
     picking = (row_blocks[:, None] == col_blocks[None, :]).astype(jnp.float32)
     row_part = jnp.einsum("kj,jab->kab", picking, received[:, 0], precision=lax.Precision.HIGHEST)
     row_sum = lax.psum(row_part, "col")

time: 594 us -> 781 us (1.31)
  waiting for transfers between devices: 205 us -> 375 us
  other arithmetic: 17.4 us -> 41 us
  matrix products: 255 us -> 240 us
  starting transfers between devices: 0.08 us -> 11.9 us
    ppermute x0 -> x9, waiting for transfers between devices: none -> 343 us  [slot_factors(): received = received + lax.ppermute(received, 'row', route)]
    psum x1 -> x0, waiting for transfers between devices: 174 us -> none  [slot_factors(): received = lax.psum(slots, 'row')]
    add x0 -> x9, other arithmetic: none -> 14.3 us  [slot_factors(): received = received + lax.ppermute(received, 'row', route)]
    dot_general x3, matrix products: 23.5 us -> 11.5 us  [slot_factors(): jnp.einsum('jw,wxab->jxab', placing, stacked, precision=lax.Precision.HIG...]
    ppermute x0 -> x9, starting transfers between devices: none -> 11.8 us  [slot_factors(): received = received + lax.ppermute(received, 'row', route)]
    another operation x3, other arithmetic: 5.3 us -> 14.6 us  [slot_factors(): stacked = jnp.stack([left_own, right_own], axis=1)]
  transfers between devices with their start and end apart: 2 -> 10, of which waited for: 2 -> 5; matrix products, arithmetic and copies ran while one was open for 16% -> 19% of each run, Pallas kernels for 0% -> 0%
where the time goes in v1:
time: 781 us; the launch traced here: 771 us
  waiting for transfers between devices  375 us (48%)
  matrix products  240 us (31%)
  local copies, waits for them, and re-layouts  88.5 us (11%)
  other arithmetic  41 us (5%)
  between operations  14.8 us (2%)
  starting transfers between devices  11.9 us (2%)
    ppermute x9, waiting for transfers between devices, slot_factors(): received = received + lax.ppermute(received, 'row', route)  343 us
    dot_general x12, matrix products, cols_update(): jnp.einsum('aibm,bml->aibl', matrix, factor, precision=lax.Precision.HIGH...  139 us
    dot_general x6, matrix products, rows_update(): jnp.einsum('aij,aibl->ajbl', factor, matrix, precision=lax.Precision.HIGH...  85.8 us
    unnamed x36, local copies, waits for them, and re-layouts  42.4 us
    psum x1, waiting for transfers between devices, slot_factors(): row_sum = lax.psum(row_part, 'col')  31.8 us
  transfers between devices with their start and end apart: 10, of which 5 were waited for; matrix products, arithmetic and copies ran while one was open for 19% of the time, Pallas kernels for 0%

profile of v1, /device:TPU:0, one launch (start us, length us, event | category | flops | bytes accessed | tf_op | source)
XLA Modules:
  0.0 771.2 jit_solution(9803722542023548085)
XLA Ops:
  14.6 6.4 gather_fusion.4
  21.0 6.4 gather_fusion.5
  44.6 4.3 fusion.46
  58.5 10.4 %fusion.65 = (f32[2,1,256,256]{3,0,2,1:T(2,128)S(1)}, f32[2,1,256,256]{3,0,2,1:T(2,128)S(1)}) fusion(f32[2,256,256]{2,1,0:T(8,128)S(1)} %bitcast.246, pred[2,256]{0,1:T(8,128)(4,1)S(1)} %copy.101, f32[2,256,256]{2,1,0:T(8,128)S(1)} %bitcast.249), kind=kLoop, calls=%fused_computation.99 | loop fusion | flops 262144 | bytes 2097664 | tf_op jit(solution)/shard_map/stack | solution.py:35
  85.8 84.7 %collective-permute-done.7 = f32[8,2,256,256]{3,0,2,1:T(8,128)S(1)} collective-permute-done((f32[8,2,256,256]{3,0,2,1:T(8,128)S(1)}, f32[8,2,256,256]{3,0,2,1:T(8,128)S(1)}, u32[]{:S(2)}, u32[]{:S(2)}) %collective-permute-start.7) | collective-permute-done | bytes 4194336 | tf_op jit(solution)/shard_map/ppermute | solution.py:41
  173.1 87.2 %collective-permute-done.4 = f32[8,2,256,256]{3,0,2,1:T(8,128)S(1)} collective-permute-done((f32[8,2,256,256]{3,0,2,1:T(8,128)S(1)}, f32[8,2,256,256]{3,0,2,1:T(8,128)S(1)}, u32[]{:S(2)}, u32[]{:S(2)}) %collective-permute-start.4) | collective-permute-done | bytes 4194336 | tf_op jit(solution)/shard_map/ppermute | solution.py:41
  263.0 87.1 %collective-permute-done.1 = f32[8,2,256,256]{3,0,2,1:T(8,128)} collective-permute-done((f32[8,2,256,256]{3,0,2,1:T(8,128)S(1)}, f32[8,2,256,256]{3,0,2,1:T(8,128)}, u32[]{:S(2)}, u32[]{:S(2)}) %collective-permute-start.1) | collective-permute-done | bytes 4194336 | tf_op jit(solution)/shard_map/ppermute | solution.py:41
  361.3 84.3 %collective-permute-done.2 = f32[8,2,256,256]{3,0,2,1:T(8,128)S(1)} collective-permute-done((f32[8,2,256,256]{3,0,2,1:T(8,128)S(1)}, f32[8,2,256,256]{3,0,2,1:T(8,128)S(1)}, u32[]{:S(2)}, u32[]{:S(2)}) %collective-permute-start.2) | collective-permute-done | bytes 4194336 | tf_op jit(solution)/shard_map/ppermute | solution.py:41
  449.4 8.5 %fusion.31 = (f32[8,256,256,1]{2,0,1,3:T(8,128)}, f32[8,256,256,1]{2,0,1,3:T(8,128)}, f32[8,256,256,1]{2,0,1,3:T(8,128)}, f32[8,256,256,1]{2,0,1,3:T(8,128)S(1)}...) fusion(f32[8,2,256,256]{3,0,2,1:T(8,128)} %copy-done.7, f32[256,256]{1,0:T(8,128)S(1)} %fusion.78, ...), kind=kLoop, calls=%fused_computation.41 | loop fusion | flops 4718592 | bytes 25428064 | tf_op jit(solution)/shard_map/add | solution.py:22
  457.9 21.2 %fusion.22 = f32[8,256,4,256]{3,1,2,0:T(8,128)} fusion(f32[4,256,8,256]{3,2,1,0:T(8,128)} %param.11, f32[8,256,256,1]{2,0,1,3:T(8,128)S(1)} %get-tuple-element.58), kind=kOutput, calls=%fused_computation.28 | convolution fusion | flops 6442450944 | bytes 18874368 | tf_op jit(solution)/shard_map/aibm,bml->aibl/dot_general | solution.py:30
  479.2 12.7 %fusion.6 = f32[8,256,4,256]{3,1,2,0:T(8,128)} fusion(f32[8,256,4,256]{3,1,2,0:T(8,128)} %fusion.22, f32[8,256,256,1]{2,0,1,3:T(8,128)S(1)} %get-tuple-element.60), kind=kOutput, calls=%fused_computation.12 | convolution fusion | flops 6442450944 | bytes 18874368 | tf_op jit(solution)/shard_map/aibm,bml->aibl/dot_general | solution.py:30
  499.7 15.8 %fusion.24 = f32[4,256,8,256]{1,3,0,2:T(8,128)} fusion(f32[8,256,4,256]{3,1,2,0:T(8,128)} %fusion.6, f32[8,256,256,1]{2,0,1,3:T(8,128)} %get-tuple-element.42), kind=kOutput, calls=%fused_computation.30 | convolution fusion | flops 6442450944 | bytes 18874368 | tf_op jit(solution)/shard_map/aibm,bml->aibl/dot_general | solution.py:30
  515.5 10.4 %copy.155 = f32[4,256,8,256]{3,2,1,0:T(8,128)} copy(f32[4,256,8,256]{1,3,0,2:T(8,128)} %fusion.24) | data formatting | bytes 16777216
  526.0 14.8 %fusion.20 = f32[8,256,4,256]{3,1,2,0:T(8,128)S(1)} fusion(f32[8,256,256,1]{1,2,3,0:T(8,128)} %copy.163, f32[4,256,8,256]{3,2,1,0:T(8,128)} %param.12), kind=kOutput, calls=%fused_computation.26 | convolution fusion | flops 6442450944 | bytes 18874368 | tf_op jit(solution)/shard_map/aibm,bml->aibl/dot_general | solution.py:30
  540.7 8.8 %fusion.2 = f32[8,256,4,256]{3,1,2,0:T(8,128)S(1)} fusion(f32[8,256,256,1]{1,2,3,0:T(8,128)S(1)} %copy-done, f32[8,256,4,256]{3,1,2,0:T(8,128)S(1)} %fusion.20), kind=kOutput, calls=%fused_computation.8 | convolution fusion | flops 6442450944 | bytes 18874368 | tf_op jit(solution)/shard_map/aibm,bml->aibl/dot_general | solution.py:30
  549.6 9.8 %fusion.27 = f32[4,256,8,256]{1,3,0,2:T(8,128)} fusion(f32[8,256,256,1]{1,2,3,0:T(8,128)S(1)} %copy.170, f32[8,256,4,256]{3,1,2,0:T(8,128)S(1)} %fusion.2), kind=kOutput, calls=%fused_computation.31 | convolution fusion | flops 6442450944 | bytes 18874368 | tf_op jit(solution)/shard_map/aibm,bml->aibl/dot_general | solution.py:30
  559.4 10.4 %copy.156 = f32[4,256,8,256]{3,2,1,0:T(8,128)} copy(f32[4,256,8,256]{1,3,0,2:T(8,128)} %fusion.27) | data formatting | bytes 16777216
  569.8 31.8 %all-reduce.3.cloned.1.call-done = (f32[4,256,256]{2,1,0:T(8,128)}, f32[4,256,256]{2,1,0:T(8,128)}, f32[4,256,256]{2,1,0:T(8,128)}) async-done(((f32[4,256,256]{2,1,0:T(8,128)}, f32[4,256,256]{2,1,0:T(8,128)}, f32[4,256,256]{2,1,0:T(8,128)}), (f32[4,256,256]{2,1,0:T(8,128)}, f32[4,256,256]{2,1,0:T(8,128)}, f32[4,256,256]{2,1,0:T(8,128)})) %all-reduce.3.cloned.1.call-update) | async-done | bytes 3145744 | tf_op jit(solution)/shard_map/psum | solution.py:44
  601.6 14.4 %fusion.18 = f32[4,256,8,256]{3,1,0,2:T(8,128)S(1)} fusion(f32[4,256,8,256]{3,2,1,0:T(8,128)} %param.9, f32[4,256,256]{2,1,0:T(8,128)} %get-tuple-element.27, f32[4]{0:T(128)S(1)} %get-tuple-element.82, f32[256,256]{1,0:T(8,128)S(1)} %fusion.78), kind=kOutput, calls=%fused_computation.24 | convolution fusion | flops 6442975232 | bytes 18087952 | tf_op jit(solution)/shard_map/aij,aibl->ajbl/dot_general | solution.py:26
  616.1 8.9 %fusion.118 = f32[8,256,4,256]{3,1,2,0:T(8,128)S(1)} fusion(f32[8,256,256,1]{1,2,3,0:T(8,128)S(1)} %copy-done.3, f32[4,256,8,256]{3,1,0,2:T(8,128)S(1)} %fusion.18), kind=kOutput, calls=%fused_computation.195 | convolution fusion | flops 6442450944 | bytes 18874368 | tf_op jit(solution)/shard_map/aibm,bml->aibl/dot_general | solution.py:30
  625.0 14.3 %fusion.16 = f32[4,256,8,256]{3,1,0,2:T(8,128)S(1)} fusion(f32[8,256,4,256]{3,1,2,0:T(8,128)S(1)} %fusion.118, f32[4,256,256]{2,1,0:T(8,128)S(1)} %copy-done.9, f32[4]{0:T(128)S(1)} %get-tuple-element.83, f32[256,256]{1,0:T(8,128)S(1)} %fusion.78), kind=kOutput, calls=%fused_computation.22 | convolution fusion | flops 6442975232 | bytes 18087952 | tf_op jit(solution)/shard_map/aij,aibl->ajbl/dot_general | solution.py:26
  639.3 9.3 %fusion.119 = f32[8,256,4,256]{3,1,2,0:T(8,128)S(1)} fusion(f32[8,256,256,1]{1,2,3,0:T(8,128)S(1)} %copy-done.1, f32[4,256,8,256]{3,1,0,2:T(8,128)S(1)} %fusion.16), kind=kOutput, calls=%fused_computation.196 | convolution fusion | flops 6442450944 | bytes 18874368 | tf_op jit(solution)/shard_map/aibm,bml->aibl/dot_general | solution.py:30
  648.6 14.2 %fusion.14 = f32[4,256,8,256]{3,1,0,2:T(8,128)S(1)} fusion(f32[8,256,4,256]{3,1,2,0:T(8,128)S(1)} %fusion.119, f32[4,256,256]{2,1,0:T(8,128)S(1)} %copy-done.8, f32[256,256]{1,0:T(8,128)S(1)} %fusion.78, f32[4]{0:T(128)S(1)} %broadcast_subtract_fusion.2), kind=kOutput, calls=%fused_computation.20 | convolution fusion | flops 6442975232 | bytes 18087952 | tf_op jit(solution)/shard_map/aij,aibl->ajbl/dot_general | solution.py:26
  662.8 9.7 %convolution_bitcast_fusion.1 = f32[4,256,8,256]{1,3,0,2:T(8,128)} fusion(f32[8,256,256,1]{1,2,3,0:T(8,128)S(1)} %copy.170, f32[4,256,8,256]{3,1,0,2:T(8,128)S(1)} %fusion.14), kind=kOutput, calls=%fused_computation.33 | convolution fusion | flops 6442450944 | bytes 18874368 | tf_op jit(solution)/shard_map/aibm,bml->aibl/dot_general | solution.py:30
  672.5 10.4 %copy.153 = f32[4,256,8,256]{3,2,1,0:T(8,128)} copy(f32[4,256,8,256]{1,3,0,2:T(8,128)} %convolution_bitcast_fusion.1) | data formatting | bytes 16777216
  682.9 14.4 %fusion.12 = f32[4,256,8,256]{3,1,0,2:T(8,128)S(1)} fusion(f32[4,256,8,256]{3,2,1,0:T(8,128)} %param.10, f32[4,256,256]{2,1,0:T(8,128)} %get-tuple-element.27, f32[4]{0:T(128)S(1)} %get-tuple-element.82, f32[256,256]{1,0:T(8,128)S(1)} %fusion.78), kind=kOutput, calls=%fused_computation.18 | convolution fusion | flops 6442975232 | bytes 18087952 | tf_op jit(solution)/shard_map/aij,aibl->ajbl/dot_general | solution.py:26
  697.4 8.9 %fusion.120 = f32[8,256,4,256]{3,1,2,0:T(8,128)S(1)} fusion(f32[8,256,256,1]{1,2,3,0:T(8,128)S(1)} %copy-done.4, f32[4,256,8,256]{3,1,0,2:T(8,128)S(1)} %fusion.12), kind=kOutput, calls=%fused_computation.197 | convolution fusion | flops 6442450944 | bytes 18874368 | tf_op jit(solution)/shard_map/aibm,bml->aibl/dot_general | solution.py:30
  706.3 14.3 %fusion.10 = f32[4,256,8,256]{3,1,0,2:T(8,128)S(1)} fusion(f32[8,256,4,256]{3,1,2,0:T(8,128)S(1)} %fusion.120, f32[4,256,256]{2,1,0:T(8,128)S(1)} %copy-done.10, f32[4]{0:T(128)S(1)} %get-tuple-element.83, f32[256,256]{1,0:T(8,128)S(1)} %fusion.78), kind=kOutput, calls=%fused_computation.16 | convolution fusion | flops 6442975232 | bytes 18087952 | tf_op jit(solution)/shard_map/aij,aibl->ajbl/dot_general | solution.py:26
  720.5 9.3 %fusion.121 = f32[8,256,4,256]{3,1,2,0:T(8,128)S(1)} fusion(f32[8,256,256,1]{1,2,3,0:T(8,128)S(1)} %copy-done.2, f32[4,256,8,256]{3,1,0,2:T(8,128)S(1)} %fusion.10), kind=kOutput, calls=%fused_computation.198 | convolution fusion | flops 6442450944 | bytes 18874368 | tf_op jit(solution)/shard_map/aibm,bml->aibl/dot_general | solution.py:30
  729.8 14.2 %fusion.8 = f32[4,256,8,256]{3,1,0,2:T(8,128)S(1)} fusion(f32[8,256,4,256]{3,1,2,0:T(8,128)S(1)} %fusion.121, f32[4,256,256]{2,1,0:T(8,128)S(1)} %copy-done.8, f32[256,256]{1,0:T(8,128)S(1)} %fusion.78, f32[4]{0:T(128)S(1)} %broadcast_subtract_fusion.2), kind=kOutput, calls=%fused_computation.14 | convolution fusion | flops 6442975232 | bytes 18087952 | tf_op jit(solution)/shard_map/aij,aibl->ajbl/dot_general | solution.py:26
  744.1 9.7 %convolution_bitcast_fusion = f32[4,256,8,256]{1,3,0,2:T(8,128)} fusion(f32[8,256,256,1]{1,2,3,0:T(8,128)S(1)} %copy.170, f32[4,256,8,256]{3,1,0,2:T(8,128)S(1)} %fusion.8), kind=kOutput, calls=%fused_computation.32 | convolution fusion | flops 6442450944 | bytes 18874368 | tf_op jit(solution)/shard_map/aibm,bml->aibl/dot_general | solution.py:30
  753.8 10.4 %copy.154 = f32[4,256,8,256]{3,2,1,0:T(8,128)} copy(f32[4,256,8,256]{1,3,0,2:T(8,128)} %convolution_bitcast_fusion) | data formatting | bytes 16777216
  (119 shorter events, 79.0 us)
Async XLA Ops:
  7.2 3.2 copy-start.12
  7.2 3.2 copy-start.13
  7.2 594.4 %all-reduce.3.cloned.1.call-start = ((), (), s32[]{:S(2)}) async-start(), calls=%async_computation | async-start | bytes 6291456 | tf_op jit(solution)/shard_map/psum | solution.py:44
  21.0 6.4 copy-start.11
  34.7 37.7 %collective-permute-start.6 = (f32[8,2,256,256]{3,0,2,1:T(8,128)}, f32[8,2,256,256]{3,0,2,1:T(8,128)}, u32[]{:S(2)}, u32[]{:S(2)}) collective-permute-start(f32[8,2,256,256]{3,0,2,1:T(8,128)} %fusion.50), channel_id=1, source_target_pairs={{0,4},{4,0},{8,12},{12,8},{16,20},{20,16},{24,28},{28,24},{1,5},{5... | collective-permute-start | bytes 12582920 | tf_op jit(solution)/shard_map/ppermute | solution.py:41
  48.9 30.1 %collective-permute-start.3 = (f32[8,2,256,256]{3,0,2,1:T(8,128)}, f32[8,2,256,256]{3,0,2,1:T(8,128)}, u32[]{:S(2)}, u32[]{:S(2)}) collective-permute-start(f32[8,2,256,256]{3,0,2,1:T(8,128)} %fusion.46), channel_id=1, source_target_pairs={{0,4},{4,0},{8,12},{12,8},{16,20},{20,16},{24,28},{28,24},{1,5},{5... | collective-permute-start | bytes 12582920 | tf_op jit(solution)/shard_map/ppermute | solution.py:41
  71.9 11.3 %collective-permute-start = (f32[8,2,256,256]{3,0,2,1:T(8,128)S(1)}, f32[8,2,256,256]{3,0,2,1:T(8,128)S(1)}, u32[]{:S(2)}, u32[]{:S(2)}) collective-permute-start(f32[8,2,256,256]{3,0,2,1:T(8,128)S(1)} %fusion.42), channel_id=1, source_target_pairs={{0,4},{4,0},{8,12},{12,8},{16,20},{20,16},{24,28},{28,24},{1,5},{5... | collective-permute-start | bytes 12582920 | tf_op jit(solution)/shard_map/ppermute | solution.py:41
  76.4 94.0 %collective-permute-start.7 = (f32[8,2,256,256]{3,0,2,1:T(8,128)S(1)}, f32[8,2,256,256]{3,0,2,1:T(8,128)S(1)}, u32[]{:S(2)}, u32[]{:S(2)}) collective-permute-start(f32[8,2,256,256]{3,0,2,1:T(8,128)S(1)} %add.161), channel_id=1, source_target_pairs={{0,8},{4,12},{8,0},{12,4},{16,24},{20,28},{24,16},{28,20},{1,9},{5... | collective-permute-start | bytes 12582920 | tf_op jit(solution)/shard_map/ppermute | solution.py:41
  83.0 177.3 %collective-permute-start.4 = (f32[8,2,256,256]{3,0,2,1:T(8,128)S(1)}, f32[8,2,256,256]{3,0,2,1:T(8,128)S(1)}, u32[]{:S(2)}, u32[]{:S(2)}) collective-permute-start(f32[8,2,256,256]{3,0,2,1:T(8,128)S(1)} %add.153), channel_id=1, source_target_pairs={{0,8},{4,12},{8,0},{12,4},{16,24},{20,28},{24,16},{28,20},{1,9},{5... | collective-permute-start | bytes 12582920 | tf_op jit(solution)/shard_map/ppermute | solution.py:41
  83.7 266.4 %collective-permute-start.1 = (f32[8,2,256,256]{3,0,2,1:T(8,128)S(1)}, f32[8,2,256,256]{3,0,2,1:T(8,128)}, u32[]{:S(2)}, u32[]{:S(2)}) collective-permute-start(f32[8,2,256,256]{3,0,2,1:T(8,128)S(1)} %add.143), channel_id=1, source_target_pairs={{0,8},{4,12},{8,0},{12,4},{16,24},{20,28},{24,16},{28,20},{1,9},{5... | collective-permute-start | bytes 12582920 | tf_op jit(solution)/shard_map/ppermute | solution.py:41
  171.0 184.4 %collective-permute-start.8 = (f32[8,2,256,256]{3,0,2,1:T(8,128)S(1)}, f32[8,2,256,256]{3,0,2,1:T(8,128)S(1)}, u32[]{:S(2)}, u32[]{:S(2)}) collective-permute-start(f32[8,2,256,256]{3,0,2,1:T(8,128)S(1)} %add.162), channel_id=1, source_target_pairs={{0,16},{4,20},{8,24},{12,28},{16,0},{20,4},{24,8},{28,12},{1,17},{... | collective-permute-start | bytes 12582920 | tf_op jit(solution)/shard_map/ppermute | solution.py:41
  260.9 97.5 %collective-permute-start.5 = (f32[8,2,256,256]{3,0,2,1:T(8,128)S(1)}, f32[8,2,256,256]{3,0,2,1:T(8,128)S(1)}, u32[]{:S(2)}, u32[]{:S(2)}) collective-permute-start(f32[8,2,256,256]{3,0,2,1:T(8,128)S(1)} %add.154), channel_id=1, source_target_pairs={{0,16},{4,20},{8,24},{12,28},{16,0},{20,4},{24,8},{28,12},{1,17},{... | collective-permute-start | bytes 12582920 | tf_op jit(solution)/shard_map/ppermute | solution.py:41
  353.1 92.4 %collective-permute-start.2 = (f32[8,2,256,256]{3,0,2,1:T(8,128)S(1)}, f32[8,2,256,256]{3,0,2,1:T(8,128)S(1)}, u32[]{:S(2)}, u32[]{:S(2)}) collective-permute-start(f32[8,2,256,256]{3,0,2,1:T(8,128)S(1)} %add.144), channel_id=1, source_target_pairs={{0,16},{4,20},{8,24},{12,28},{16,0},{20,4},{24,8},{28,12},{1,17},{... | collective-permute-start | bytes 12582920 | tf_op jit(solution)/shard_map/ppermute | solution.py:41
  355.9 3.0 copy-start.5
  358.9 87.2 %copy-start.6 = (f32[8,2,256,256]{3,0,2,1:T(8,128)}, f32[8,2,256,256]{3,0,2,1:T(8,128)S(1)}, u32[]{:S(2)}) copy-start(f32[8,2,256,256]{3,0,2,1:T(8,128)S(1)} %add.155) | copy-start | bytes 12582916
  446.1 2.0 copy-start.7
  526.0 14.8 %copy-start = (f32[8,256,256,1]{1,2,3,0:T(8,128)S(1)}, f32[8,256,256,1]{1,2,3,0:T(8,128)}, u32[]{:S(2)}) copy-start(f32[8,256,256,1]{1,2,3,0:T(8,128)} %copy.167) | copy-start | bytes 6291460
  601.6 14.4 %copy-start.3 = (f32[8,256,256,1]{1,2,3,0:T(8,128)S(1)}, f32[8,256,256,1]{1,2,3,0:T(8,128)}, u32[]{:S(2)}) copy-start(f32[8,256,256,1]{1,2,3,0:T(8,128)} %copy.163) | copy-start | bytes 6291460
  616.0 8.9 %copy-start.9 = (f32[4,256,256]{2,1,0:T(8,128)S(1)}, f32[4,256,256]{2,1,0:T(8,128)}, u32[]{:S(2)}) copy-start(f32[4,256,256]{2,1,0:T(8,128)} %get-tuple-element.28) | copy-start | bytes 3145732
  625.0 14.3 %copy-start.1 = (f32[8,256,256,1]{1,2,3,0:T(8,128)S(1)}, f32[8,256,256,1]{1,2,3,0:T(8,128)}, u32[]{:S(2)}) copy-start(f32[8,256,256,1]{1,2,3,0:T(8,128)} %copy.167) | copy-start | bytes 6291460
  639.2 9.3 %copy-start.8 = (f32[4,256,256]{2,1,0:T(8,128)S(1)}, f32[4,256,256]{2,1,0:T(8,128)}, u32[]{:S(2)}) copy-start(f32[4,256,256]{2,1,0:T(8,128)} %get-tuple-element.29) | copy-start | bytes 3145732
  682.9 14.4 %copy-start.4 = (f32[8,256,256,1]{1,2,3,0:T(8,128)S(1)}, f32[8,256,256,1]{1,2,3,0:T(8,128)}, u32[]{:S(2)}) copy-start(f32[8,256,256,1]{1,2,3,0:T(8,128)} %copy.163) | copy-start | bytes 6291460
  697.3 8.9 %copy-start.10 = (f32[4,256,256]{2,1,0:T(8,128)S(1)}, f32[4,256,256]{2,1,0:T(8,128)}, u32[]{:S(2)}) copy-start(f32[4,256,256]{2,1,0:T(8,128)} %get-tuple-element.28) | copy-start | bytes 3145732
  706.3 14.3 %copy-start.2 = (f32[8,256,256,1]{1,2,3,0:T(8,128)S(1)}, f32[8,256,256,1]{1,2,3,0:T(8,128)}, u32[]{:S(2)}) copy-start(f32[8,256,256,1]{1,2,3,0:T(8,128)} %copy.167) | copy-start | bytes 6291460
Sparse Core Ops, SparseCore 0:
  479.3 122.2 all-reduce.2
